TPU v7x, 512 devices: a whole 4x4x16 slice. The times are simulated.
512 devices in a mesh: ctx: 16 (over x_lo, y, core), ep: 32 (over z, x_hi).
Axes of the slice: x: 4 (x_hi: 2, x_lo: 2; x = x_hi * 2 + x_lo), y: 4, z: 16, core: 2. Of those that a mesh axis runs over, the one named last changes fastest.
Arguments:
- queries: bfloat16 [2048, 73728], P('ctx', 'ep'), may hold values from -12 to 12
- latent: bfloat16 [2048, 576], P('ctx'), may hold values from -5 to 5
- doc_ids: int32 [2048], replicated, may hold values from 0 to 3, never falling along the last dimension, each value on 1 to 1024 neighbouring positions
- w_uv: bfloat16 [128, 512, 128], P('ep'), may hold values from -0.75 to 0.75
- w_out: bfloat16 [16384, 7168], P('ep', 'ctx'), may hold values from -0.046875 to 0.046875
- hidden_in: bfloat16 [2048, 7168], P('ep', 'ctx'), may hold values from -24 to 24
- norm_gain: float32 [7168], P('ctx'), may hold values from 0.5 to 1.5
- route_ids: int32 [2048, 8], P('ep'), may hold values from 0 to 31, all different within a row; in each aligned block of 64 rows (0 to 63, 64 to 127, ...) at most 18 rows name the same one
- route_weights: float32 [2048, 8], P('ep'), may hold values from 0.1 to 1
- w_gate: bfloat16 [32, 7168, 1024], P('ep', 'ctx'), may hold values from -0.0625 to 0.0625
- w_up: bfloat16 [32, 7168, 1024], P('ep', 'ctx'), may hold values from -0.0625 to 0.0625
- w_down: bfloat16 [32, 1024, 7168], P('ep', None, 'ctx'), may hold values from -0.1875 to 0.1875
Outputs:
- layer_output: bfloat16 [2048, 7168], P('ep', 'ctx')
Inputs may be any that keep to these rules, and one draw needn't show every extreme that they name: `doc_ids`: document numbers never fall along the sequence; a document has at most 1024 tokens, and one has exactly that many. `route_ids`: each token names 8 different experts; among the 64 tokens of one index of ep no expert is named by more than 18 tokens, a bound that some block reaches.
All inputs are finite; a program needn't handle non-finite values.
Results may differ from a plain program's by a relative error of at most 0.014.
Values may be sent and summed in bfloat16 or wider, within the bound.
A program may use at most 64 MiB of HBM per device.

v0:
```python
import math

import jax
import jax.numpy as jnp
from jax import lax
from jax.sharding import PartitionSpec as P

D = 7168
KVL = 512


score_scale = (1.0 + 0.1 * math.log(40.0)) ** 2 / math.sqrt(192.0)
masked_score = -1e30


def attend_group(state, query_block, query_first, keys, key_first, doc_ids):
    count = query_block.shape[0]
    key_count = keys.shape[0]
    running_max, running_total, running_sum = state

    def update(unused):
        scores = (
            jnp.einsum("nhc,kc->hnk", query_block, keys, preferred_element_type=jnp.float32)
            * score_scale
        )
        query_pos = query_first + jnp.arange(count, dtype=jnp.int32)
        key_pos = jnp.arange(key_count, dtype=jnp.int32)
        query_doc = lax.dynamic_slice_in_dim(doc_ids, query_first, count)
        allowed = (key_pos[None, :] <= query_pos[:, None]) & (
            doc_ids[None, :] == query_doc[:, None]
        )
        scores = jnp.where(allowed[None], scores, masked_score)
        new_max = jnp.maximum(running_max, jnp.max(scores, axis=2))
        probs = jnp.where(allowed[None], jnp.exp(scores - new_max[:, :, None]), 0.0)
        new_total = jnp.sum(probs, axis=2)
        values = keys[:, :KVL]
        new_sum = jnp.einsum(
            "hnk,kc->hnc", probs.astype(jnp.bfloat16), values, preferred_element_type=jnp.float32
        )
        return (new_max, new_total, new_sum)

    return lax.cond(key_first > query_first + count - 1, lambda unused: state, update, 0)


def shards(
    queries,
    latent,
    doc_ids,
    w_uv,
    w_out,
    hidden_in,
    norm_gain,
    route_ids,
    route_weights,
    w_gate,
    w_up,
    w_down,
):
    ctx_rank = lax.axis_index("ctx")
    block_rows = queries.shape[0]
    head_count = w_uv.shape[0]
    key_width = latent.shape[1]
    heads_local = queries.reshape(block_rows, head_count, key_width)
    own_first = ctx_rank * block_rows
    groups = ((heads_local, own_first),)

    def start_state(query_block):
        count = query_block.shape[0]
        return (
            jnp.full((head_count, count), masked_score, jnp.float32),
            jnp.zeros((head_count, count), jnp.float32),
            jnp.zeros((head_count, count, KVL), jnp.float32),
        )

    def add_keys(states, keys, key_first):
        return tuple(
            (
                attend_group(state, group[0], group[1], keys, key_first, doc_ids)
                for state, group in zip(states, groups)
            )
        )

    initial = tuple((start_state(group[0]) for group in groups))
    states = add_keys(initial, lax.all_gather(latent, "ctx", axis=0, tiled=True), jnp.int32(0))
    context = jnp.concatenate(
        [(state[2] / state[1][:, :, None]).astype(jnp.bfloat16) for state in states], axis=1
    )
    head_values = jnp.einsum("hnc,hcv->nhv", context, w_uv, preferred_element_type=jnp.float32)
    head_values = head_values.reshape(block_rows, -1).astype(jnp.bfloat16)
    partial_value = jnp.dot(
        lax.all_gather(head_values, "ctx", axis=0, tiled=True),
        w_out,
        preferred_element_type=jnp.float32,
    )
    attended = lax.psum_scatter(
        partial_value.astype(jnp.bfloat16), "ep", scatter_dimension=0, tiled=True
    ).astype(jnp.float32)
    residual = hidden_in.astype(jnp.float32) + attended
    squares = lax.psum(jnp.sum(residual * residual, axis=1), "ctx")
    normed = (residual * lax.rsqrt(squares / D + 1e-06)[:, None] * norm_gain).astype(jnp.bfloat16)
    expert_count = lax.axis_size("ep")
    token_count = hidden_in.shape[0]
    top_count = route_ids.shape[1]
    capacity = min(token_count, max(2, token_count * top_count * 9 // (8 * expert_count)))
    pair_count = token_count * top_count
    flat_ids = route_ids.reshape(pair_count)
    chosen = (flat_ids[:, None] == jnp.arange(expert_count, dtype=jnp.int32)[None, :]).astype(
        jnp.bfloat16
    )
    pair_index = jnp.arange(pair_count, dtype=jnp.int32)
    earlier = (pair_index[:, None] > pair_index[None, :]).astype(jnp.bfloat16)
    before = jnp.dot(earlier, chosen, preferred_element_type=jnp.float32)
    slot = jnp.sum(before * chosen.astype(jnp.float32), axis=1).astype(jnp.int32)
    target = flat_ids * capacity + slot
    placing = (
        jnp.arange(expert_count * capacity, dtype=jnp.int32)[:, None] == target[None, :]
    ).astype(jnp.bfloat16)
    repeated = jnp.repeat(normed, top_count, axis=0)
    outgoing = jnp.dot(placing, repeated, preferred_element_type=jnp.float32).astype(jnp.bfloat16)
    outgoing = outgoing.reshape(expert_count, capacity, -1)
    arrived = lax.all_to_all(outgoing, "ep", split_axis=0, concat_axis=0, tiled=True)
    source_count, item_count, width = arrived.shape
    flat_rows = arrived.reshape(source_count * item_count, width)
    gate_part = jnp.dot(flat_rows, w_gate[0], preferred_element_type=jnp.float32)
    up_part = jnp.dot(flat_rows, w_up[0], preferred_element_type=jnp.float32)
    both = jnp.stack([gate_part, up_part], axis=1)
    both = lax.psum(both.astype(jnp.bfloat16), "ctx").astype(jnp.float32)
    activated = (jax.nn.silu(both[:, 0]) * both[:, 1]).astype(jnp.bfloat16)
    produced = jnp.dot(activated, w_down[0], preferred_element_type=jnp.float32).astype(
        jnp.bfloat16
    )
    processed = produced.reshape(source_count, item_count, -1)
    incoming = lax.all_to_all(processed, "ep", split_axis=0, concat_axis=0, tiled=True)
    gathered_rows = lax.dot_general(
        placing,
        incoming.reshape(expert_count * capacity, -1),
        (((0,), (0,)), ((), ())),
        preferred_element_type=jnp.float32,
    )
    mixture = jnp.sum(
        gathered_rows.reshape(token_count, top_count, -1) * route_weights[:, :, None], axis=1
    )
    return (residual + mixture).astype(jnp.bfloat16)


def solution(mesh):
    return jax.shard_map(
        shards,
        mesh=mesh,
        in_specs=(
            P("ctx", "ep"),
            P("ctx", None),
            P(),
            P("ep", None, None),
            P("ep", "ctx"),
            P("ep", "ctx"),
            P("ctx"),
            P("ep", None),
            P("ep", None),
            P("ep", "ctx", None),
            P("ep", "ctx", None),
            P("ep", None, "ctx"),
        ),
        out_specs=P("ep", "ctx"),
        check_vma=False,
    )
```

profile of v0, /device:TPU:6, one launch (start us, length us, event | category | flops | bytes accessed | tf_op | source)
XLA Modules:
  0.0 1072.0 jit_solution(10790732302764875122)
XLA Ops:
  6.5 0.0 copy-start
  6.5 0.0 all-gather.3.cloned.1.call-start
  6.5 1.8 copy.23
  8.3 0.0 all-gather.3.cloned.1.call-update
  8.4 0.0 all-gather.5.cloned.1.call-start
  8.4 47.6 %all-gather.3.cloned.1.call-done = bf16[2048,576]{1,0:T(8,128)(2,1)} async-done(((bf16[128,576]{1,0:T(8,128)(2,1)}), bf16[2048,576]{1,0:T(8,128)(2,1)}) %all-gather.3.cloned.1.call-update) | async-done | bytes 2359312 | tf_op jit(solution)/shard_map/all_gather | solution.py:84
  56.0 9.6 conditional.1
  56.0 0.8 dynamic_slice.2
  56.8 1.0 fusion.14
  57.9 1.4 copy.24
  59.3 0.0 copy-start.6
  59.3 3.9 fusion
  63.2 0.0 copy-done.6
  63.2 1.4 fusion.5
  64.6 1.0 fusion.2
  65.6 0.0 copy-start.10
  65.6 0.0 copy-done.9
  65.6 1.1 convolution_convert_fusion.5
  66.7 0.0 all-gather.5.cloned.1.call-update
  66.7 0.0 copy-start.3
  66.8 0.0 reduce-scatter.2.cloned.1.call-start
  66.8 45.5 %all-gather.5.cloned.1.call-done = bf16[2048,512]{0,1:T(8,128)(2,1)} async-done(((bf16[128,512]{0,1:T(8,128)(2,1)}), bf16[2048,512]{0,1:T(8,128)(2,1)}) %all-gather.5.cloned.1.call-update) | async-done | bytes 2097168 | tf_op jit(solution)/shard_map/all_gather | solution.py:91
  112.3 0.0 copy-done.10
  112.3 4.2 convolution_convert_fusion
  116.5 0.0 copy-start.1
  116.5 0.0 reduce-scatter.2.cloned.1.call-update
  116.6 0.0 all-reduce.2.cloned.1.call-start
  116.6 0.0 copy-done.3
  116.6 0.1 copy.26
  116.7 0.1 reshape.119
  116.8 0.3 fusion.28
  117.1 665.9 %reduce-scatter.2.cloned.1.call-done = bf16[64,448]{1,0:T(8,128)(2,1)} async-done(((bf16[2048,448]{1,0:T(8,128)(2,1)}), bf16[64,448]{1,0:T(8,128)(2,1)}) %reduce-scatter.2.cloned.1.call-update) | async-done | bytes 57360 | tf_op jit(solution)/shard_map/reduce_scatter | solution.py:95
  783.0 0.0 copy-done.1
  783.0 1.0 multiply_reduce_fusion
  783.9 27.2 %psum.14 = f32[64]{0:T(128)S(1)} all-reduce(f32[64]{0:T(128)S(1)} %multiply_reduce_fusion), channel_id=1, replica_groups=mesh['ctx'=16,'ep'=32] {'ctx'}, use_global_device_ids=true, to_apply=%region_7.8 | all-reduce | flops 64 | bytes 512 | tf_op jit(solution)/shard_map/psum | solution.py:99
  811.1 0.0 copy-done.5
  811.1 0.9 multiply_convert_fusion
  812.0 0.6 convolution_convert_fusion.3
  812.7 0.2 copy.27
  812.9 0.2 reshape.121
  813.1 54.9 %all_to_all.10 = bf16[32,18,448]{2,1,0:T(8,128)(2,1)S(1)} all-to-all(bf16[32,18,448]{2,1,0:T(8,128)(2,1)S(1)} %reshape.121), channel_id=1, replica_groups=mesh['ctx'=16,'ep'=32] {'ep'}, dimensions={0} | all-to-all | bytes 1032192 | tf_op jit(solution)/shard_map/all_to_all | solution.py:121
  868.1 0.3 reshape.122
  868.4 0.0 copy-done
  868.4 0.8 fusion.19
  869.2 0.0 copy-done.7
  869.2 0.8 fusion.20
  870.0 1.6 pad_maximum_fusion
  871.6 0.0 all-reduce.2.cloned.1.call-update
  871.7 0.0 copy-start.8
  871.7 128.4 %all-reduce.2.cloned.1.call-done = bf16[576,2,1024]{2,0,1:T(8,128)(2,1)} async-done(((bf16[576,2,1024]{2,0,1:T(8,128)(2,1)}), bf16[576,2,1024]{2,0,1:T(8,128)(2,1)}) %all-reduce.2.cloned.1.call-update) | async-done | bytes 2359312 | tf_op jit(solution)/shard_map/psum | solution.py:127
  1000.1 2.2 convert_element_type.77
  1002.3 0.0 copy-done.8
  1002.3 1.1 convolution_convert_fusion.4
  1003.4 0.0 copy-start.4
  1003.4 0.2 copy.28
  1003.7 1.1 reshape.123
  1004.8 15.4 %all-to-all-start.1 = ((bf16[32,18,448]{2,1,0:T(8,128)(2,1)}), bf16[32,18,448]{2,1,0:T(8,128)(2,1)S(1)}, u32[]{:S(2)}, u32[]{:S(2)}) async-start(bf16[32,18,448]{2,1,0:T(8,128)(2,1)} %reshape.123), calls=%async_computation.2 | async-start | bytes 1572864 | tf_op jit(solution)/shard_map/all_to_all | solution.py:133
  1020.2 0.0 copy-done.4
  1020.2 0.1 copy.30
  1020.3 43.4 %all-to-all-done.1 = bf16[32,18,448]{2,1,0:T(8,128)(2,1)S(1)} async-done(((bf16[32,18,448]{2,1,0:T(8,128)(2,1)}), bf16[32,18,448]{2,1,0:T(8,128)(2,1)S(1)}, u32[]{:S(2)}, u32[]{:S(2)}) %all-to-all-start.1) | async-done | bytes 516128 | tf_op jit(solution)/shard_map/all_to_all | solution.py:133
  1063.7 0.3 reshape.124
  1064.0 0.8 fusion.23
  1064.8 0.0 copy-done.2
  1064.8 0.7 add_convert_fusion
  (8 shorter events, 0.0 us)
Async XLA Ops:
  6.5 861.9 %copy-start = (bf16[1,448,1024]{2,1,0:T(8,128)(2,1)S(1)}, bf16[1,448,1024]{2,1,0:T(8,128)(2,1)}, u32[]{:S(2)}) copy-start(bf16[1,448,1024]{2,1,0:T(8,128)(2,1)} %param.23) | copy-start | bytes 2752516
  6.5 49.5 %all-gather.3.cloned.1.call-start = ((), (), s32[]{:S(2)}) async-start(), calls=%async_computation.3 | async-start | bytes 2785280 | tf_op jit(solution)/shard_map/all_gather | solution.py:84
  8.4 104.0 %all-gather.5.cloned.1.call-start = ((), (), s32[]{:S(2)}) async-start(), calls=%async_computation.4 | async-start | bytes 2228224 | tf_op jit(solution)/shard_map/all_gather | solution.py:91
  56.0 9.6 copy-start.9
  59.3 3.9 copy-start.6
  65.6 46.7 %copy-start.10 = (bf16[512,448]{0,1:T(8,128)(2,1)S(1)}, bf16[512,448]{0,1:T(8,128)(2,1)}, u32[]{:S(2)}) copy-start(bf16[512,448]{0,1:T(8,128)(2,1)} %param.18) | copy-start | bytes 1376260
  66.7 49.9 %copy-start.3 = (s32[64,8]{0,1:T(8,128)S(1)}, s32[64,8]{0,1:T(8,128)}, u32[]{:S(2)}) copy-start(s32[64,8]{0,1:T(8,128)} %param.21) | copy-start | bytes 6148
  66.8 716.2 %reduce-scatter.2.cloned.1.call-start = ((), (), s32[]{:S(2)}) async-start(), calls=%async_computation.5 | async-start | bytes 2162688 | tf_op jit(solution)/shard_map/reduce_scatter | solution.py:95
  116.5 666.4 %copy-start.1 = (bf16[64,448]{1,0:T(8,128)(2,1)S(1)}, bf16[64,448]{1,0:T(8,128)(2,1)}, u32[]{:S(2)}) copy-start(bf16[64,448]{1,0:T(8,128)(2,1)} %param.19) | copy-start | bytes 172036
  116.5 694.6 %copy-start.5 = (f32[448]{0:T(512)S(1)}, f32[448]{0:T(512)}, u32[]{:S(2)}) copy-start(f32[448]{0:T(512)} %param.20) | copy-start | bytes 5380
  116.6 883.6 %all-reduce.2.cloned.1.call-start = ((), (), s32[]{:S(2)}) async-start(), calls=%async_computation.6 | async-start | bytes 4718592 | tf_op jit(solution)/shard_map/psum | solution.py:127
  868.1 1.2 copy-start.7
  871.7 130.6 %copy-start.8 = (bf16[1,1024,448]{1,2,0:T(8,128)(2,1)S(1)}, bf16[1,1024,448]{1,2,0:T(8,128)(2,1)}, u32[]{:S(2)}) copy-start(bf16[1,1024,448]{1,2,0:T(8,128)(2,1)} %param.25) | copy-start | bytes 2752516
  1003.4 16.8 %copy-start.4 = (f32[64,8]{0,1:T(8,128)S(1)}, f32[64,8]{0,1:T(8,128)}, u32[]{:S(2)}) copy-start(f32[64,8]{0,1:T(8,128)} %param.22) | copy-start | bytes 6148
  1004.8 60.0 %copy-start.2 = (bf16[64,448]{1,0:T(8,128)(2,1)S(1)}, bf16[64,448]{1,0:T(8,128)(2,1)}, u32[]{:S(2)}) copy-start(bf16[64,448]{1,0:T(8,128)(2,1)} %reduce-scatter.2.cloned.1.call-done) | copy-start | bytes 172036
  1004.8 58.9 %all-to-all-start.1 = ((bf16[32,18,448]{2,1,0:T(8,128)(2,1)}), bf16[32,18,448]{2,1,0:T(8,128)(2,1)S(1)}, u32[]{:S(2)}, u32[]{:S(2)}) async-start(bf16[32,18,448]{2,1,0:T(8,128)(2,1)} %reshape.123), calls=%async_computation.2 | async-start | bytes 1572864 | tf_op jit(solution)/shard_map/all_to_all | solution.py:133
Sparse Core Ops, SparseCore 0:
  9.5 46.4 all-gather.2
  66.9 45.4 all-gather.4
  116.7 666.2 reduce-scatter.1
  871.8 128.2 all-reduce.1
where the time goes:
time: 1070 us
  waiting for transfers between devices  931 us (87%)
  blocking collectives  82.1 us (8%)
  starting transfers between devices  15.6 us (1%)
  matrix products  14.9 us (1%)
  between operations  13.3 us (1%)
    reduce_scatter x1, waiting for transfers between devices, shards(): lax.psum_scatter(partial_value.astype(jnp.bfloat16), 'ep', scatter_dimens...  666 us
    psum x1, waiting for transfers between devices, shards(): both = lax.psum(both.astype(jnp.bfloat16), 'ctx').astype(jnp.float32)  128 us
    all_to_all x1, blocking collectives, shards(): lax.all_to_all(outgoing, 'ep', split_axis=0, concat_axis=0, tiled=True)  54.9 us
    all_gather x1, waiting for transfers between devices, shards(): lax.all_gather(latent, 'ctx', axis=0, tiled=True)  47.6 us
    all_gather x1, waiting for transfers between devices, shards(): lax.all_gather(head_values, 'ctx', axis=0, tiled=True)  45.5 us
    all_to_all x1, waiting for transfers between devices, shards(): lax.all_to_all(processed, 'ep', split_axis=0, concat_axis=0, tiled=True)  43.4 us
    psum x1, blocking collectives, shards(): squares = lax.psum(jnp.sum(residual * residual, axis=1), 'ctx')  27.2 us
  transfers between devices with their start and end apart: 5, of which 5 were waited for; matrix products, arithmetic and copies ran while one was open for 0% of the time, Pallas kernels for 0%

commit v1 on v0

v1 whole, which is shorter than its diff:
```python
import math

import jax
import jax.numpy as jnp
from jax import lax
from jax.experimental import pallas as pl
from jax.experimental.pallas import tpu as pltpu
from jax.sharding import PartitionSpec as P

D = 7168
KVL = 512
KW = 576
HEADS_DEV = 4
VDIM = 128
NX, NY, NK = 2, 4, 2
NZ, NXH = 16, 2
N_CTX = NX * NY * NK
BLK = 128
BACK = 8
TOK = 64
FEAT = 448
NT = (((1,), (1,)), ((), ()))

score_scale = (1.0 + 0.1 * math.log(40.0)) ** 2 / math.sqrt(192.0)
masked_score = -1e30


class Place:
    def __init__(self):
        self.c = lax.axis_index("ctx")
        self.e = lax.axis_index("ep")
        self.k = lax.rem(self.c, NK)
        self.y = lax.rem(self.c // NK, NY)
        self.x = self.c // (NK * NY)
        self.z = self.e // NXH
        self.h = lax.rem(self.e, NXH)

    def ctx(self, dx, dy, dk):
        x = lax.rem(self.x + dx + NX, NX)
        y = lax.rem(self.y + dy + NY, NY)
        k = lax.rem(self.k + dk + NK, NK)
        return (x * NY + y) * NK + k

    def ep(self, dz, dh):
        z = lax.rem(self.z + dz + NZ, NZ)
        h = lax.rem(self.h + dh + NXH, NXH)
        return z * NXH + h


def remote(src, dst, send, recv, device):
    return pltpu.make_async_remote_copy(
        src_ref=src, dst_ref=dst, send_sem=send, recv_sem=recv,
        device_id=device, device_id_type=pl.DeviceIdType.MESH,
    )


def entry_barrier(devices):
    barrier = pltpu.get_barrier_semaphore()
    for device in devices:
        pl.semaphore_signal(barrier, inc=1, device_id=device, device_id_type=pl.DeviceIdType.MESH)
    pl.semaphore_wait(barrier, len(devices))


CHIPS = [(dx, dy) for dy in (2, 1, 3, 0) for dx in (1, 0) if (dx, dy) != (0, 0)]


def attention_kernel(
    q_ref, lat_ref, doc_ref, wuv_ref, wo_ref, hid_ref, out_ref,
    kt, qs, allow, hv, rr, rl, sr, sl, pr, plft, xs, xr,
    lat_send, lat_recv, hv_send, hv_fwd, hv_recv, zr_send, zr_recv, zl_send, zl_recv, x_sem,
):
    at = Place()
    c, e, z, h = at.c, at.e, at.z, at.h
    peers = [(lax.rem(c + i, N_CTX), e) for i in range(1, N_CTX)]
    right, left, cross = (c, at.ep(1, 0)), (c, at.ep(-1, 0)), (c, at.ep(0, 1))
    entry_barrier(peers + [right, left, cross])

    def latent_copy(d, target):
        return remote(lat_ref, kt.at[:, pl.ds(d * BLK, BLK)], lat_send.at[d - 1], lat_recv.at[d - 1], target)

    for d in range(BACK, 0, -1):
        @pl.when(c + d < N_CTX)
        def _():
            latent_copy(d, (lax.rem(c + d, N_CTX), e)).start()

    kt[:, 0:BLK] = lat_ref[...]
    for n in range(HEADS_DEV):
        qs[n] = q_ref[:, n * KW:(n + 1) * KW]
    own = jnp.broadcast_to(doc_ref[pl.ds(c, 1), :].astype(jnp.float32), (BLK, BLK))
    query_doc = own.T
    rows = lax.broadcasted_iota(jnp.int32, (BLK, BLK), 0)
    cols = lax.broadcasted_iota(jnp.int32, (BLK, BLK), 1)
    allow[:, 0:BLK] = jnp.where((cols <= rows) & (own == query_doc), 1.0, 0.0)
    for d in range(1, BACK + 1):
        key_doc = doc_ref[pl.ds(lax.rem(c - d + N_CTX, N_CTX), 1), :].astype(jnp.float32)
        key_doc = jnp.where(c - d >= 0, key_doc, -1.0)
        allow[:, d * BLK:(d + 1) * BLK] = jnp.where(key_doc == query_doc, 1.0, 0.0)

    for d in range(1, BACK + 1):
        @pl.when(c - d >= 0)
        def _():
            latent_copy(d, (c, e)).wait_recv()

        @pl.when(c - d < 0)
        def _():
            kt[:, pl.ds(d * BLK, BLK)] = jnp.zeros((KW, BLK), jnp.bfloat16)

    @pl.loop(0, HEADS_DEV)
    def _(n):
        allowed = allow[...] > 0.5
        scores = jnp.dot(qs[n], kt[...], preferred_element_type=jnp.float32) * score_scale
        scores = jnp.where(allowed, scores, masked_score)
        peak = jnp.max(scores, axis=1, keepdims=True)
        probs = jnp.where(allowed, jnp.exp(scores - peak), 0.0)
        total = jnp.sum(probs, axis=1, keepdims=True)
        mixed = lax.dot_general(probs.astype(jnp.bfloat16), kt[0:KVL, :], NT, preferred_element_type=jnp.float32)
        context = (mixed / total).astype(jnp.bfloat16)
        value = jnp.dot(context, wuv_ref[n], preferred_element_type=jnp.float32)
        hv[c, :, pl.ds(pl.multiple_of(n * VDIM, VDIM), VDIM)] = value.astype(jnp.bfloat16)

    def value_copy(slot, send, target):
        return remote(hv.at[slot], hv.at[slot], send, hv_recv.at[slot], target)

    for i, (dx, dy) in enumerate(CHIPS):
        value_copy(c, hv_send.at[i], (at.ctx(dx, dy, 0), e)).start()
    mate = (at.ctx(0, 0, 1), e)
    value_copy(c, hv_send.at[7], mate).start()
    for i, (dx, dy) in reversed(list(enumerate(CHIPS))):
        slot = at.ctx(-dx, -dy, 0)
        value_copy(slot, hv_fwd.at[i], mate).wait_recv()
        value_copy(slot, hv_fwd.at[i], mate).start()
    value_copy(at.ctx(0, 0, 1), hv_send.at[7], mate).wait_recv()
    for i, (dx, dy) in reversed(list(enumerate(CHIPS))):
        slot = at.ctx(-dx, -dy, 1)
        value_copy(slot, hv_fwd.at[i], mate).wait_recv()

    def chunk(t):
        return lax.dot_general(hv[t], wo_ref[...], NT, preferred_element_type=jnp.float32)

    theirs = pl.multiple_of((1 - h) * TOK, TOK)
    mine = pl.multiple_of(h * TOK, TOK)

    def hop(rightward, s, half, start):
        if rightward:
            return remote(sr.at[s, pl.ds(start, TOK)], rr.at[s, pl.ds(start, TOK)],
                          zr_send.at[2 * s + half], zr_recv.at[2 * s + half], right)
        return remote(sl.at[s, pl.ds(start, TOK)], rl.at[s, pl.ds(start, TOK)],
                      zl_send.at[2 * s + half], zl_recv.at[2 * s + half], left)

    for s in range(8):
        pr[...] = chunk(lax.rem(z + 8 - s, NZ))
        if s < 7:
            plft[...] = chunk(lax.rem(z + 9 + s, NZ))
        for half, start in ((0, theirs), (1, mine)):
            here = pl.ds(start, TOK)
            value = pr[here, :]
            if s > 0:
                hop(True, s - 1, half, start).wait_recv()
                value = value + rr[s - 1, here, :].astype(jnp.float32)
            sr[s, here, :] = value.astype(jnp.bfloat16)
            hop(True, s, half, start).start()
            if s < 7:
                value = plft[here, :]
                if s > 0:
                    hop(False, s - 1, half, start).wait_recv()
                    value = value + rl[s - 1, here, :].astype(jnp.float32)
                sl[s, here, :] = value.astype(jnp.bfloat16)
                hop(False, s, half, start).start()
    pr[...] = chunk(z)
    for half, start in ((0, theirs), (1, mine)):
        here = pl.ds(start, TOK)
        hop(False, 6, half, start).wait_recv()
        value = pr[here, :] + rl[6, here, :].astype(jnp.float32)
        hop(True, 7, half, start).wait_recv()
        value = value + rr[7, here, :].astype(jnp.float32)
        if half == 0:
            xs[...] = value.astype(jnp.bfloat16)
            swap = remote(xs, xr, x_sem.at[0], x_sem.at[1], cross)
            swap.start()
        else:
            swap.wait_recv()
            out_ref[...] = hid_ref[...].astype(jnp.float32) + (value + xr[...].astype(jnp.float32))

    swap.wait_send()
    for d in range(BACK, 0, -1):
        @pl.when(c + d < N_CTX)
        def _():
            latent_copy(d, (c, e)).wait_send()
    for i in range(len(CHIPS)):
        value_copy(c, hv_send.at[i], mate).wait_send()
        value_copy(c, hv_fwd.at[i], mate).wait_send()
    value_copy(c, hv_send.at[7], mate).wait_send()
    for s in range(8):
        for half, start in ((0, theirs), (1, mine)):
            hop(True, s, half, start).wait_send()
            if s < 7:
                hop(False, s, half, start).wait_send()


def attention_part(queries, latent, doc_ids, w_uv, w_out, hidden_in):
    vmem = pl.BlockSpec(memory_space=pltpu.VMEM)
    bf, f32 = jnp.bfloat16, jnp.float32
    dma = pltpu.SemaphoreType.DMA
    return pl.pallas_call(
        attention_kernel,
        out_shape=jax.ShapeDtypeStruct((TOK, FEAT), f32),
        in_specs=[vmem] * 6,
        out_specs=vmem,
        scratch_shapes=[
            pltpu.VMEM((KW, (BACK + 1) * BLK), bf),
            pltpu.VMEM((HEADS_DEV, BLK, KW), bf),
            pltpu.VMEM((BLK, (BACK + 1) * BLK), f32),
            pltpu.VMEM((N_CTX, BLK, HEADS_DEV * VDIM), bf),
            pltpu.VMEM((8, BLK, FEAT), bf),
            pltpu.VMEM((7, BLK, FEAT), bf),
            pltpu.VMEM((8, BLK, FEAT), bf),
            pltpu.VMEM((7, BLK, FEAT), bf),
            pltpu.VMEM((BLK, FEAT), f32),
            pltpu.VMEM((BLK, FEAT), f32),
            pltpu.VMEM((TOK, FEAT), bf),
            pltpu.VMEM((TOK, FEAT), bf),
            dma((8,)), dma((8,)), dma((8,)), dma((7,)), dma((16,)),
            dma((16,)), dma((16,)), dma((14,)), dma((14,)), dma((2,)),
        ],
        compiler_params=pltpu.CompilerParams(
            collective_id=0, has_side_effects=True, vmem_limit_bytes=48 << 20
        ),
    )(queries, latent.T, doc_ids.reshape(N_CTX, BLK), w_uv, w_out.T, hidden_in)


HALF = 288
SPAN = NZ * TOK
ROWS = 2 * HALF
PIECE = ROWS // NY
QUART = 256
FF = 1024
TOP = 8
EP_STEPS = [(dz, dh) for dz in range(NZ) for dh in range(NXH) if (dz, dh) != (0, 0)]


def silu(v):
    return v / (1.0 + jnp.exp(-v))


def moe_kernel(
    res_ref, gain_ref, ids_ref, wts_ref, wg_ref, wu_ref, wd_ref, out_ref,
    route, tabs, s_own, s_mate, s_far, t_own, t_mate, w_col, r_col, sq, rs_all, r_rows, xs, picked, far_in,
    g, rk, yb, yf, ys, xsend, xb, act, yw, y_far, prod, rr, rl, sr, sl,
    route_send, route_recv, sq_send, sq_recv, r_send, r_recv, ar_send, ar_recv, al_send, al_recv, px_sem,
    k_send, k_recv, y_send, y_recv, gx_sem, a_send, a_recv, bx_sem, zr_send, zr_recv, zl_send, zl_recv,
):
    bf, f32 = jnp.bfloat16, jnp.float32
    at = Place()
    c, e, x, y, k, z, h = at.c, at.e, at.x, at.y, at.k, at.z, at.h
    right, left, cross = (c, at.ep(1, 0)), (c, at.ep(-1, 0)), (c, at.ep(0, 1))
    mate, side = (at.ctx(0, 0, 1), e), (at.ctx(1, 0, 0), e)
    ahead, behind = (at.ctx(0, 1, 0), e), (at.ctx(0, -1, 0), e)
    ep_peers = [(c, at.ep(dz, dh)) for dz, dh in EP_STEPS]
    ctx_peers = [(lax.rem(c + i, N_CTX), e) for i in range(1, N_CTX)]
    entry_barrier(ep_peers + ctx_peers)

    def route_copy(i, slot, target):
        return remote(route.at[slot], route.at[slot], route_send.at[i], route_recv.at[slot], target)

    route[e, 0:8, :] = ids_ref[...].astype(f32)
    route[e, 8:16, :] = wts_ref[...]
    for i in range(len(EP_STEPS)):
        route_copy(i, e, ep_peers[i]).start()

    res = res_ref[...]
    part = jnp.broadcast_to(jnp.sum(res * res, axis=1, keepdims=True), (TOK, 128))
    sq[c] = part.T[0:8, :]

    def sq_copy(i, slot, target):
        return remote(sq.at[slot], sq.at[slot], sq_send.at[i], sq_recv.at[slot], target)

    for i in range(1, N_CTX):
        sq_copy(i - 1, c, ctx_peers[i - 1]).start()

    xs[z] = (res * gain_ref[...]).astype(bf)

    def pass_on(rightward, s):
        slot = lax.rem(z + NZ - s, NZ) if rightward else lax.rem(z + s, NZ)
        if rightward:
            return remote(xs.at[slot], xs.at[slot], ar_send.at[s], ar_recv.at[s], right)
        return remote(xs.at[slot], xs.at[slot], al_send.at[s], al_recv.at[s], left)

    def arrived(rightward, s):
        slot = lax.rem(z + NZ - s - 1, NZ) if rightward else lax.rem(z + s + 1, NZ)
        if rightward:
            return remote(xs.at[slot], xs.at[slot], ar_send.at[s], ar_recv.at[s], right)
        return remote(xs.at[slot], xs.at[slot], al_send.at[s], al_recv.at[s], left)

    pass_on(True, 0).start()
    pass_on(False, 0).start()

    for dz, dh in EP_STEPS:
        slot = at.ep(dz, dh)
        route_copy(0, slot, mate).wait_recv()
    mate_e = at.ep(0, 1)
    for n in range(NZ):
        near = route[n * NXH + h]
        far = route[n * NXH + (1 - h)]
        lanes = slice(n * TOK, (n + 1) * TOK)
        own_hit = jnp.where(near[0:8] == e.astype(f32), 1.0, 0.0)
        mate_hit = jnp.where(near[0:8] == mate_e.astype(f32), 1.0, 0.0)
        far_hit = jnp.where(far[0:8] == e.astype(f32), 1.0, 0.0)
        tabs[0:1, lanes] = jnp.sum(own_hit, axis=0, keepdims=True)
        tabs[1:2, lanes] = jnp.sum(mate_hit, axis=0, keepdims=True)
        tabs[2:3, lanes] = jnp.sum(far_hit, axis=0, keepdims=True)
        tabs[3:4, lanes] = jnp.sum(own_hit * near[8:16], axis=0, keepdims=True)
        tabs[4:5, lanes] = jnp.sum(far_hit * far[8:16], axis=0, keepdims=True)
        tabs[5:8, lanes] = jnp.zeros((3, TOK), f32)
    tri = jnp.where(
        lax.broadcasted_iota(jnp.int32, (128, 128), 0) < lax.broadcasted_iota(jnp.int32, (128, 128), 1), 1.0, 0.0
    ).astype(bf)
    base = jnp.zeros((8, 1), f32)
    w_own = jnp.zeros((HALF, 1), f32)
    w_far = jnp.zeros((HALF, 1), f32)
    for n in range(SPAN // 128):
        lanes = slice(n * 128, (n + 1) * 128)
        hit = tabs[:, lanes]
        rank = jnp.dot(hit.astype(bf), tri, preferred_element_type=f32) + base
        base = base + jnp.sum(hit, axis=1, keepdims=True)
        slot = jnp.where(hit > 0.5, rank, -1.0)
        row = lax.broadcasted_iota(jnp.int32, (HALF, 128), 0).astype(f32)
        pick_own = jnp.where(slot[0:1] == row, 1.0, 0.0)
        pick_far = jnp.where(slot[2:3] == row, 1.0, 0.0)
        s_own[:, lanes] = pick_own.astype(bf)
        s_mate[:, lanes] = jnp.where(slot[1:2] == row, 1.0, 0.0).astype(bf)
        s_far[:, lanes] = pick_far.astype(bf)
        w_own = w_own + jnp.sum(pick_own * tabs[3:4, lanes], axis=1, keepdims=True)
        w_far = w_far + jnp.sum(pick_far * tabs[4:5, lanes], axis=1, keepdims=True)
        col = lax.broadcasted_iota(jnp.int32, (128, HALF), 1).astype(f32)
        own_col = jnp.broadcast_to(slot[0:1], (128, 128)).T[:, 0:1]
        mate_col = jnp.broadcast_to(slot[1:2], (128, 128)).T[:, 0:1]
        t_own[lanes, :] = jnp.where(own_col == col, 1.0, 0.0).astype(bf)
        t_mate[lanes, :] = jnp.where(mate_col == col, 1.0, 0.0).astype(bf)
    w_col[0:HALF, :] = jnp.broadcast_to(w_own, (HALF, 128))
    w_col[HALF:ROWS, :] = jnp.broadcast_to(w_far, (HALF, 128))

    for i in range(1, N_CTX):
        sq_copy(0, lax.rem(c + i, N_CTX), mate).wait_recv()
    total = sq[0]
    for i in range(1, N_CTX):
        total = total + sq[i]
    rs_all[e] = lax.rsqrt(total / D + 1e-06)

    def r_copy(i, slot, target):
        return remote(rs_all.at[slot], rs_all.at[slot], r_send.at[i], r_recv.at[slot], target)

    for i in range(len(EP_STEPS)):
        r_copy(i, e, ep_peers[i]).start()

    for s in range(8):
        arrived(True, s).wait_recv()
        if s < 7:
            pass_on(True, s + 1).start()
            arrived(False, s).wait_recv()
            if s < 6:
                pass_on(False, s + 1).start()

    flat = xs[...].reshape(SPAN, FEAT)
    picked[HALF:ROWS, :] = jnp.dot(s_mate[...], flat, preferred_element_type=f32).astype(bf)
    swap = remote(picked.at[pl.ds(HALF, HALF)], far_in, px_sem.at[0], px_sem.at[1], cross)
    swap.start()
    picked[0:HALF, :] = jnp.dot(s_own[...], flat, preferred_element_type=f32).astype(bf)

    for dz, dh in EP_STEPS:
        r_copy(0, at.ep(dz, dh), mate).wait_recv()
    for n in range(NZ):
        lanes = slice(n * TOK, (n + 1) * TOK)
        r_rows[0:1, lanes] = rs_all[n * NXH + h][0:1, 0:TOK]
        r_rows[1:2, lanes] = rs_all[n * NXH + (1 - h)][0:1, 0:TOK]
    r_col[0:HALF, :] = jnp.broadcast_to(
        jnp.sum(s_own[...].astype(f32) * r_rows[0:1, :], axis=1, keepdims=True), (HALF, 128))
    r_col[HALF:ROWS, :] = jnp.broadcast_to(
        jnp.sum(s_far[...].astype(f32) * r_rows[1:2, :], axis=1, keepdims=True), (HALF, 128))

    def terms(source, first, q):
        rows = pl.ds(first, HALF)
        cols = pl.ds(pl.multiple_of(q * QUART, QUART), QUART)
        scale = r_col[rows, 0:1]
        value = source[...] if first else source[0:HALF, :]
        g[q, rows, 0:QUART] = (jnp.dot(value, wg_ref[:, cols], preferred_element_type=f32) * scale).astype(bf)
        g[q, rows, QUART:2 * QUART] = (jnp.dot(value, wu_ref[:, cols], preferred_element_type=f32) * scale).astype(bf)

    def k_copy(xx, first):
        i = 2 * xx + (1 if first else 0)
        return remote(g.at[xx * NK + (1 - k), pl.ds(first, HALF)], rk.at[xx, pl.ds(first, HALF)],
                      k_send.at[i], k_recv.at[i], mate)

    for source, first in ((picked, 0), (far_in, HALF)):
        if first:
            swap.wait_recv()
        for xx in range(NX):
            terms(source, first, xx * NK + (1 - k))
            k_copy(xx, first).start()
        for xx in range(NX):
            terms(source, first, xx * NK + k)

    for first in (0, HALF):
        for xx in range(NX):
            k_copy(xx, first).wait_recv()

    def pair_sum(xx, yy):
        rows = pl.ds(pl.multiple_of(yy * PIECE, 16), PIECE)
        return g[xx * NK + k, rows, :].astype(f32) + rk[xx, rows, :].astype(f32)

    y_up, y_down, y_over = lax.rem(y + 1, NY), lax.rem(y + 3, NY), lax.rem(y + 2, NY)

    def y_copy(i):
        dst = [yb.at[0], yb.at[1], yf.at[0, 1], yf.at[1, 0], yf.at[0, 0], yf.at[1, 1]][i]
        return remote(ys.at[i], dst, y_send.at[i], y_recv.at[i], ahead if i % 2 == 0 else behind)

    def y_put(i, value):
        ys[i] = value.astype(bf)
        y_copy(i).start()

    y_put(0, pair_sum(0, y_over))
    y_put(1, pair_sum(1, y_over))
    y_put(2, pair_sum(1, y_up))
    y_put(3, pair_sum(0, y_down))
    y_copy(0).wait_recv()
    y_put(4, pair_sum(0, y_up) + yb[0].astype(f32))
    y_copy(1).wait_recv()
    y_put(5, pair_sum(1, y_down) + yb[1].astype(f32))
    for i in range(2, 6):
        y_copy(i).wait_recv()

    def full_sum(xx):
        return pair_sum(xx, y) + yf[0, xx].astype(f32) + yf[1, xx].astype(f32)

    xsend[...] = full_sum(1 - x).astype(bf)
    gx = remote(xsend, xb, gx_sem.at[0], gx_sem.at[1], side)
    gx.start()
    sums = full_sum(x)
    gx.wait_recv()
    sums = sums + xb[...].astype(f32)
    done = (silu(sums[:, 0:QUART]) * sums[:, QUART:2 * QUART]).astype(bf)

    def spot(dx, dy, dk):
        xx, yy, kk = lax.rem(x + dx, NX), lax.rem(y + dy + NY, NY), lax.rem(k + dk, NK)
        ref = act.at[pl.ds(pl.multiple_of(yy * PIECE, 16), PIECE), pl.ds(pl.multiple_of((xx * NK + kk) * QUART, QUART), QUART)]
        return ref, (xx * NY + yy) * NK + kk

    act[pl.ds(pl.multiple_of(y * PIECE, 16), PIECE), pl.ds(pl.multiple_of((x * NK + k) * QUART, QUART), QUART)] = done
    sent = []

    def give(dx, dy, target):
        ref, slot = spot(dx, dy, 0)
        copy = remote(ref, ref, a_send.at[len(sent)], a_recv.at[slot], target)
        copy.start()
        sent.append(copy)

    def take(dx, dy, dk):
        ref, slot = spot(dx, dy, dk)
        remote(ref, ref, a_send.at[0], a_recv.at[slot], mate).wait_recv()

    for target in (side, ahead, behind, mate):
        give(0, 0, target)
    take(1, 0, 0)
    for target in (ahead, behind, mate):
        give(1, 0, target)
    for dx in range(NX):
        for dy in (-1, 1):
            take((dx + 0), dy, 0)
            if (dx, dy) == (0, -1):
                give(0, -1, ahead)
            if (dx, dy) == (1, 1):
                give(1, 1, behind)
            give(dx, dy, mate)
    for dx in range(NX):
        take(dx, 2, 0)
        give(dx, 2, mate)
    for dy in (0, -1, 1, 2):
        for dx in range(NX):
            take(dx, dy, 1)

    def down(first):
        value = lax.dot_general(act[first:first + HALF, :], wd_ref[...], NT, preferred_element_type=f32)
        yw[first:first + HALF, :] = (value * w_col[first:first + HALF, 0:1]).astype(bf)

    down(HALF)
    back = remote(yw.at[pl.ds(HALF, HALF)], y_far, bx_sem.at[0], bx_sem.at[1], cross)
    back.start()
    down(0)
    prod[...] = jnp.dot(t_own[...], yw[0:HALF, :], preferred_element_type=f32)
    back.wait_recv()
    prod[...] += jnp.dot(t_mate[...], y_far[...], preferred_element_type=f32)

    def hop(rightward, s, half):
        part = pl.ds(half * 32, 32)
        if rightward:
            return remote(sr.at[s, part], rr.at[s, part], zr_send.at[2 * s + half], zr_recv.at[2 * s + half], right)
        return remote(sl.at[s, part], rl.at[s, part], zl_send.at[2 * s + half], zl_recv.at[2 * s + half], left)

    def block(t, half):
        return prod[pl.ds(pl.multiple_of(t * TOK + half * 32, 32), 32), :]

    for s in range(8):
        for half in range(2):
            part = pl.ds(half * 32, 32)
            value = block(lax.rem(z + 8 - s, NZ), half)
            if s > 0:
                hop(True, s - 1, half).wait_recv()
                value = value + rr[s - 1, part, :].astype(f32)
            sr[s, part, :] = value.astype(bf)
            hop(True, s, half).start()
            if s < 7:
                value = block(lax.rem(z + 9 + s, NZ), half)
                if s > 0:
                    hop(False, s - 1, half).wait_recv()
                    value = value + rl[s - 1, part, :].astype(f32)
                sl[s, part, :] = value.astype(bf)
                hop(False, s, half).start()
    for half in range(2):
        part = pl.ds(half * 32, 32)
        hop(False, 6, half).wait_recv()
        value = block(z, half) + rl[6, part, :].astype(f32)
        hop(True, 7, half).wait_recv()
        value = value + rr[7, part, :].astype(f32)
        out_ref[part, :] = (res_ref[part, :] + value).astype(bf)

    for i in range(len(EP_STEPS)):
        route_copy(i, e, mate).wait_send()
        r_copy(i, e, mate).wait_send()
    for i in range(1, N_CTX):
        sq_copy(i - 1, c, mate).wait_send()
    for s in range(8):
        pass_on(True, s).wait_send()
        if s < 7:
            pass_on(False, s).wait_send()
        for half in range(2):
            hop(True, s, half).wait_send()
            if s < 7:
                hop(False, s, half).wait_send()
    swap.wait_send()
    for first in (0, HALF):
        for xx in range(NX):
            k_copy(xx, first).wait_send()
    for i in range(6):
        y_copy(i).wait_send()
    gx.wait_send()
    for copy in sent:
        copy.wait_send()
    back.wait_send()


def moe_part(residual, norm_gain, route_ids, route_weights, w_gate, w_up, w_down):
    vmem = pl.BlockSpec(memory_space=pltpu.VMEM)
    bf, f32 = jnp.bfloat16, jnp.float32
    dma = pltpu.SemaphoreType.DMA
    shapes = [
        ((32, 16, TOK), f32), ((8, SPAN), f32),
        ((HALF, SPAN), bf), ((HALF, SPAN), bf), ((HALF, SPAN), bf), ((SPAN, HALF), bf), ((SPAN, HALF), bf),
        ((ROWS, 128), f32), ((ROWS, 128), f32), ((N_CTX, 8, TOK), f32), ((32, 8, TOK), f32), ((2, SPAN), f32),
        ((NZ, TOK, FEAT), bf), ((ROWS, FEAT), bf), ((HALF, FEAT), bf),
        ((4, ROWS, 2 * QUART), bf), ((NX, ROWS, 2 * QUART), bf), ((2, PIECE, 2 * QUART), bf),
        ((2, 2, PIECE, 2 * QUART), bf), ((6, PIECE, 2 * QUART), bf), ((PIECE, 2 * QUART), bf),
        ((PIECE, 2 * QUART), bf), ((ROWS, FF), bf), ((ROWS, FEAT), bf), ((HALF, FEAT), bf), ((SPAN, FEAT), f32),
        ((8, TOK, FEAT), bf), ((7, TOK, FEAT), bf), ((8, TOK, FEAT), bf), ((7, TOK, FEAT), bf),
    ]
    counts = [31, 32, 15, 16, 31, 32, 8, 8, 7, 7, 2, 4, 4, 6, 6, 2, 17, 16, 2, 16, 16, 14, 14]
    return pl.pallas_call(
        moe_kernel,
        out_shape=jax.ShapeDtypeStruct((TOK, FEAT), bf),
        in_specs=[vmem] * 7,
        out_specs=vmem,
        scratch_shapes=[pltpu.VMEM(s, d) for s, d in shapes] + [dma((n,)) for n in counts],
        compiler_params=pltpu.CompilerParams(
            collective_id=1, has_side_effects=True, vmem_limit_bytes=48 << 20
        ),
    )(residual, norm_gain.reshape(1, FEAT), route_ids.T, route_weights.T, w_gate[0], w_up[0], w_down[0].T)


def shards(
    queries, latent, doc_ids, w_uv, w_out, hidden_in, norm_gain, route_ids, route_weights, w_gate, w_up, w_down,
):
    residual = attention_part(queries, latent, doc_ids, w_uv, w_out, hidden_in)
    return moe_part(residual, norm_gain, route_ids, route_weights, w_gate, w_up, w_down)


def solution(mesh):
    return jax.shard_map(
        shards,
        mesh=mesh,
        in_specs=(
            P("ctx", "ep"), P("ctx", None), P(), P("ep", None, None), P("ep", "ctx"), P("ep", "ctx"),
            P("ctx"), P("ep", None), P("ep", None),
            P("ep", "ctx", None), P("ep", "ctx", None), P("ep", None, "ctx"),
        ),
        out_specs=P("ep", "ctx"),
        check_vma=False,
    )
```

time: 1070 us -> 228 us (0.21)
  waiting for transfers between devices: 931 us -> 0 us
  Pallas kernels: 0 us -> 218 us
  blocking collectives: 82.1 us -> 0 us
  starting transfers between devices: 15.6 us -> 0 us
  matrix products: 14.9 us -> 0 us
  between operations: 13.3 us -> 0.08 us
    reduce_scatter x1 -> x0, waiting for transfers between devices: 666 us -> none  [shards(): lax.psum_scatter(partial_value.astype(jnp.bfloat16), 'ep', scatter_dimens...]
    pallas_call x0 -> x2, Pallas kernels: none -> 218 us  [the longest x1 131 us: moe_part(): pl.pallas_call(moe_kernel, out_shape=jax.ShapeDtypeStruct((TOK, FEAT), bf...]
    psum x1 -> x0, waiting for transfers between devices: 128 us -> none  [shards(): both = lax.psum(both.astype(jnp.bfloat16), 'ctx').astype(jnp.float32)]
    all_gather x2 -> x0, waiting for transfers between devices: 93.1 us -> none  [the longest x1 47.6 us: shards(): lax.all_gather(latent, 'ctx', axis=0, tiled=True)]
    all_to_all x1 -> x0, blocking collectives: 54.9 us -> none  [shards(): lax.all_to_all(outgoing, 'ep', split_axis=0, concat_axis=0, tiled=True)]
    all_to_all x1 -> x0, waiting for transfers between devices: 43.4 us -> none  [shards(): lax.all_to_all(processed, 'ep', split_axis=0, concat_axis=0, tiled=True)]
    psum x1 -> x0, blocking collectives: 27.2 us -> none  [shards(): squares = lax.psum(jnp.sum(residual * residual, axis=1), 'ctx')]
    all_to_all x1 -> x0, starting transfers between devices: 15.4 us -> none  [shards(): lax.all_to_all(processed, 'ep', split_axis=0, concat_axis=0, tiled=True)]
  transfers between devices with their start and end apart: 5 -> 0, of which waited for: 5 -> 0; matrix products, arithmetic and copies ran while one was open for 0% -> 0% of each run, Pallas kernels for 0% -> 0%
where the time goes in v1:
time: 228 us; the launch traced here: 226 us
  Pallas kernels  218 us (96%)
  local copies, waits for them, and re-layouts  7.39 us (3%)
    pallas_call x1, Pallas kernels, moe_part(): pl.pallas_call(moe_kernel, out_shape=jax.ShapeDtypeStruct((TOK, FEAT), bf...  131 us
    pallas_call x1, Pallas kernels, attention_part(): pl.pallas_call(attention_kernel, out_shape=jax.ShapeDtypeStruct((TOK, FEA...  87.6 us
    unnamed x25, local copies, waits for them, and re-layouts  7.39 us

profile of v1, /device:TPU:6, one launch (start us, length us, event | category | flops | bytes accessed | tf_op | source)
XLA Modules:
  0.0 225.7 jit_solution(7970094427545355799)
XLA Ops:
  0.0 0.0 copy-start.8
  0.0 0.7 copy-done.8
  0.7 0.0 copy-start.3
  0.7 1.1 copy-done.3
  1.8 0.0 copy-start.4
  1.8 1.0 copy-done.4
  2.8 0.0 copy-start.5
  2.8 1.0 copy-done.5
  3.8 0.0 copy-start.6
  3.8 0.9 copy-done.6
  4.7 0.0 copy-start.7
  4.7 0.8 copy-done.7
  5.6 0.0 copy-start
  5.6 0.0 copy-start.1
  5.6 0.0 copy-start.9
  5.6 0.0 copy-start.10
  5.6 0.0 copy-start.11
  5.6 87.6 %shard_map.118.res_ref = f32[64,448]{1,0:T(8,128)S(1)} custom-call(bf16[128,2304]{1,0:T(8,128)(2,1)S(1)} %copy-done.3, bf16[576,128]{1,0:T(8,128)(2,1)S(1)} %bitcast.15, s32[16,128]{1,0:T(8,128)S(1)} %bitcast.16, bf16[4,512,128]{2,1,0:T(8,128)(2,1)S(1)} %copy-done.4, bf16[448,512]{1,0:T(8,128)(2,1)S(1)} %bitcast.14, bf16[64,448]{1,0:T(8,128)(2,1)S(1)} %copy-done.7), custom_call_target="tpu_custom_call" | custom-call | tf_op jit(solution)/shard_map/pallas_call | solution.py:204
  93.2 0.0 copy-done
  93.2 0.0 copy-done.1
  93.2 0.0 copy-done.9
  93.2 0.0 copy-done.10
  93.2 0.0 copy-done.11
  93.2 0.0 copy-start.2
  93.3 1.2 copy-done.2
  94.4 130.7 %shard_map.119 = bf16[64,448]{1,0:T(8,128)(2,1)S(1)} custom-call(f32[64,448]{1,0:T(8,128)S(1)} %shard_map.118.res_ref, f32[1,448]{1,0:T(1,128)S(1)} %bitcast.19, s32[8,64]{1,0:T(8,128)S(1)} %bitcast.17, f32[8,64]{1,0:T(8,128)S(1)} %bitcast.18, bf16[448,1024]{1,0:T(8,128)(2,1)S(1)} %bitcast.11, bf16[448,1024]{1,0:T(8,128)(2,1)S(1)} %bitcast.12, ...), custom_call_target="tpu_custom_call" | custom-call | tf_op jit(solution)/shard_map/pallas_call | solution.py:565
  225.1 0.6 copy.14
Async XLA Ops:
  0.0 0.7 copy-start.8
  0.7 1.1 copy-start.3
  1.8 1.0 copy-start.4
  2.8 1.0 copy-start.5
  3.8 0.9 copy-start.6
  4.7 0.8 copy-start.7
  5.6 87.6 %copy-start = (bf16[1,448,1024]{2,1,0:T(8,128)(2,1)S(1)}, bf16[1,448,1024]{2,1,0:T(8,128)(2,1)}, u32[]{:S(2)}) copy-start(bf16[1,448,1024]{2,1,0:T(8,128)(2,1)} %param.21) | copy-start | bytes 2752516
  5.6 87.6 %copy-start.1 = (bf16[1,448,1024]{2,1,0:T(8,128)(2,1)S(1)}, bf16[1,448,1024]{2,1,0:T(8,128)(2,1)}, u32[]{:S(2)}) copy-start(bf16[1,448,1024]{2,1,0:T(8,128)(2,1)} %param.22) | copy-start | bytes 2752516
  5.6 87.6 %copy-start.9 = (s32[64,8]{0,1:T(8,128)S(1)}, s32[64,8]{0,1:T(8,128)}, u32[]{:S(2)}) copy-start(s32[64,8]{0,1:T(8,128)} %param.19) | copy-start | bytes 6148
  5.6 87.6 %copy-start.10 = (f32[64,8]{0,1:T(8,128)S(1)}, f32[64,8]{0,1:T(8,128)}, u32[]{:S(2)}) copy-start(f32[64,8]{0,1:T(8,128)} %param.20) | copy-start | bytes 6148
  5.6 87.7 %copy-start.11 = (f32[448]{0:T(512)S(1)}, f32[448]{0:T(512)}, u32[]{:S(2)}) copy-start(f32[448]{0:T(512)} %param.18) | copy-start | bytes 5380
  93.2 1.2 copy-start.2
